TPU v7x, 32 devices: a whole 2x2x4 slice. The times are simulated.
32 devices in a mesh: rep: 16 (over z, x, core), dom: 2 (over y).
Axes of the slice: x: 2, y: 2, z: 4, core: 2. Of those that a mesh axis runs over, the one named last changes fastest.
Arguments:
- field: float32 [16, 256, 2048], P('rep', 'dom'), may hold values from -2.5 to 2.5
- momentum: float32 [16, 256, 2048], P('rep', 'dom'), may hold values from -4 to 4
- labels: int32 [16], P('rep'), may hold values from 0 to 15, each once
- betas: float32 [16], replicated, may hold values from 0.4 to 1.6
- accept: int32 [16], P('rep'), may hold values 0 or 1
- swap_pairs: int32 [16], replicated, may hold values from 0 to 15, as said below
Outputs:
- field_out: float32 [16, 256, 2048], P('rep', 'dom')
- field_sorted: float32 [16, 256, 2048], P('rep', 'dom')
- labels_out: int32 [16], P('rep')
- energy_change: float32 [16], P('rep')
- ladder_action: float32 [16], P('rep')
Inputs may be any that keep to these rules, and one draw needn't show every extreme that they name: Each temperature index t is paired with itself, with t - 1 or with t + 1, and the pairing is symmetric: swap_pairs[swap_pairs[t]] = t. labels is a permutation of the temperature indices.
All inputs are finite; a program needn't handle non-finite values. No bound on the sum of `accept` on one device may be relied on, other than what follows from the above.
Results may differ from a plain program's by a relative error of at most 0.0003.
Values sent between devices are 32-bit elements; how exact they have to be, the bound alone decides.
No kernel may reach another device: no remote copies, remote signals or barrier semaphores. Data moves between devices by JAX's collectives and lax.ppermute only.
A program may use at most 64 MiB of HBM per device.

v0:
```python
import jax
import jax.numpy as jnp
from jax import lax
from jax.sharding import PartitionSpec as P

STEPS = 8
hopping = 0.18
quartic = 0.3
step_size = 0.05


def with_halo(cells, sides, width):
    for axis, dim in sides:
        count = lax.axis_size(axis)
        head = lax.slice_in_dim(cells, 0, width, axis=dim)
        tail = lax.slice_in_dim(cells, cells.shape[dim] - width, cells.shape[dim], axis=dim)
        cells = jnp.concatenate(
            [
                lax.ppermute(tail, axis, [(i, (i + 1) % count) for i in range(count)]),
                cells,
                lax.ppermute(head, axis, [((i + 1) % count, i) for i in range(count)]),
            ],
            axis=dim,
        )
    return cells


def force_rows(padded, coldness):
    centre = padded[1:-1]
    beside_all = padded[:-2] + padded[2:] + (jnp.roll(centre, 1, 1) + jnp.roll(centre, -1, 1))
    return coldness * (
        -2.0 * hopping * beside_all
        + 2.0 * centre
        + 4.0 * quartic * centre * (centre * centre - 1.0)
    )


def site_terms(padded, margin, strip_rows):
    values = padded[margin : margin + strip_rows]
    lower_row = padded[margin + 1 : margin + 1 + strip_rows]
    neighbours = lower_row + jnp.roll(values, -1, 1)
    squared = values * values
    return (
        -2.0 * hopping * values * neighbours + squared + quartic * (squared - 1.0) * (squared - 1.0)
    )


def trim_rows(values, margin, target):
    excess = margin - target
    return values[excess : values.shape[0] - excess]


def info_rows(label_value, action, members, lanes):
    pair = jnp.concatenate((label_value[None], action))
    front = jnp.broadcast_to(pair[None, None, :], (members, 1, 2))
    return jnp.concatenate((front, jnp.zeros((members, 1, lanes - 2), jnp.float32)), 2)


def body(field, momentum, labels, betas, accept, swap_pairs):
    strip_rows = field.shape[1]
    width = field.shape[2]
    ladder_index = jnp.arange(betas.shape[0], dtype=jnp.int32)
    chosen = ladder_index == labels[0]
    coldness = jnp.sum(jnp.where(chosen, betas, 0.0))
    new_label = jnp.sum(jnp.where(chosen, swap_pairs, 0))
    start_field = field[0]
    start_moment = momentum[0]
    current = start_field
    moment = start_moment
    margin = 0
    old_action = None
    new_action = None
    for leap_step in range(STEPS + 1):
        if margin == 0:
            stacked = with_halo(jnp.stack((current, moment)), (("dom", 1),), 3)
            current = stacked[0]
            moment = stacked[1]
            margin = 3
        padded = current
        outer = margin
        if leap_step == 0:
            old_action = site_terms(padded, outer, strip_rows)
        if leap_step == STEPS:
            new_action = site_terms(padded, outer, strip_rows)
        force_now = force_rows(padded, coldness)
        moment = trim_rows(moment, margin, outer - 1)
        current = trim_rows(padded, outer, outer - 1)
        margin = outer - 1
        factor = 0.5 * step_size if leap_step == 0 or leap_step == STEPS else step_size
        moment = moment - factor * force_now
        if leap_step < STEPS:
            current = current + step_size * moment
    change_part = jnp.sum(
        0.5 * moment * moment
        + coldness * new_action
        - (0.5 * start_moment * start_moment + coldness * old_action)
    )
    accepted = accept[0] == 1
    action_part = jnp.where(accepted, jnp.sum(new_action), jnp.sum(old_action))
    field_out = jnp.where(accepted, current, start_field)
    label_value = new_label.astype(jnp.float32)
    change, action = lax.psum((change_part[None], action_part[None]), "dom")
    members = lax.axis_size("rep")
    blocks = field_out.reshape(members, -1, width)
    outgoing = jnp.concatenate((blocks, info_rows(label_value, action, members, width)), 1)
    spread = lax.all_to_all(
        outgoing.reshape(1, -1, width), "rep", split_axis=1, concat_axis=0, tiled=True
    )
    label_values = spread[:, -1, 0]
    actions = spread[:, -1, 1]
    received = spread[:, :-1]
    held_labels = label_values.astype(jnp.int32)
    onehot = held_labels[None, :] == ladder_index[:, None]
    holder = jnp.sum(jnp.where(onehot, ladder_index[None, :], 0), 1)
    sites_total = lax.axis_size("dom") * strip_rows * width
    ladder_all = jnp.sum(jnp.where(onehot, actions[None, :], 0.0), 1) / sites_total
    ladder = lax.dynamic_slice_in_dim(ladder_all, lax.axis_index("rep"), 1)
    ordered = jnp.take(received, holder, axis=0)
    returned = lax.all_to_all(ordered, "rep", split_axis=0, concat_axis=1, tiled=True)
    return (field_out[None], returned, new_label[None], change, ladder)


def solution(mesh):
    placed = (P("rep", "dom", None), P("rep", "dom", None), P("rep"), P(), P("rep"), P())
    return jax.shard_map(
        body,
        mesh=mesh,
        in_specs=placed,
        out_specs=(P("rep", "dom", None), P("rep", "dom", None), P("rep"), P("rep"), P("rep")),
        check_vma=False,
    )
```

profile of v0, /device:TPU:9, one launch (start us, length us, event | category | flops | bytes accessed | tf_op | source)
XLA Modules:
  0.0 129.3 jit_solution(5219297042923690402)
XLA Ops:
  0.6 1.4 %constant_dynamic-update-slice_fusion.1 = f32[2,128,2048]{2,1,0:T(8,128)S(1)} fusion(f32[1,128,2048]{2,1,0:T(8,128)} %param.6), kind=kLoop, calls=%fused_computation.139 | loop fusion | bytes 2097152
  2.0 0.1 copy-done.3
  2.3 1.3 %collective-permute-start.1 = (f32[2,3,2048]{2,1,0:T(4,128)S(1)}, f32[2,3,2048]{2,1,0:T(4,128)S(1)}, u32[]{:S(2)}, u32[]{:S(2)}) collective-permute-start(f32[2,3,2048]{2,1,0:T(4,128)S(1)} %get-tuple-element.33), channel_id=1, source_target_pairs={{1,0},{0,1},{3,2},{2,3},{5,4},{4,5},{7,6},{6,7},{9,8},{8,9},{11,10... | collective-permute-start | bytes 147464 | tf_op jit(solution)/shard_map/ppermute | solution.py:21
  3.6 0.2 collective-permute-start
  4.5 0.6 fusion.80
  5.1 0.4 collective-permute-done.1
  5.5 2.0 %collective-permute-done = f32[2,3,2048]{2,1,0:T(4,128)S(1)} collective-permute-done((f32[2,3,2048]{2,1,0:T(4,128)S(1)}, f32[2,3,2048]{2,1,0:T(4,128)S(1)}, u32[]{:S(2)}, u32[]{:S(2)}) %collective-permute-start) | collective-permute-done | bytes 49184 | tf_op jit(solution)/shard_map/ppermute | solution.py:19
  7.5 0.2 pad_maximum_fusion
  7.7 0.1 slice_bitcast_fusion.5
  7.9 0.4 fusion.109
  8.3 1.5 %multiply_add_fusion.5 = (f32[132,2048]{1,0:T(8,128)S(1)}, f32[132,2048]{1,0:T(8,128)S(1)}) fusion(f32[2,134,2048]{2,1,0:T(8,128)S(1)} %pad_maximum_fusion, f32[132,1]{1,0:T(8,128)S(1)} %get-tuple-element.70, f32[132,2047]{1,0:T(8,128)S(1)} %get-tuple-element.72, f32[132,2047]{1,0:T(8,128)S(1)} %get-tuple-element.71, f32[132,1]{1,0:T(8,128)S(1)} %get-tuple-element.69, ...), kind=kLoop, calls=%fused_computation.77 | loop fusion | flops 4866048 | bytes 8650756 | tf_op jit(solution)/shard_map/add | solution.py:92
  9.9 0.4 fusion.107
  10.3 0.1 fusion.106
  10.4 1.5 %multiply_add_fusion.4 = (f32[130,2048]{1,0:T(8,128)S(1)}, f32[130,2048]{1,0:T(8,128)S(1)}) fusion(f32[132,2048]{1,0:T(8,128)S(1)} %get-tuple-element.24, f32[130,1]{1,0:T(8,128)S(1)} %get-tuple-element.66, f32[130,2047]{1,0:T(8,128)S(1)} %get-tuple-element.68, f32[130,2047]{1,0:T(8,128)S(1)} %get-tuple-element.67, f32[130,1]{1,0:T(8,128)S(1)} %get-tuple-element.65, ...), kind=kLoop, calls=%fused_computation.76 | loop fusion | flops 4792320 | bytes 8519684 | tf_op jit(solution)/shard_map/add | solution.py:92
  11.9 0.4 fusion.105
  12.4 1.5 %add_bitcast_fusion.1 = (f32[1,128,2048]{2,1,0:T(8,128)S(1)}, f32[128,2048]{1,0:T(8,128)S(1)}) fusion(f32[130,2048]{1,0:T(8,128)S(1)} %get-tuple-element.22, f32[128,1]{1,0:T(8,128)S(1)} %get-tuple-element.62, f32[128,2047]{1,0:T(8,128)S(1)} %get-tuple-element.64, f32[128,2047]{1,0:T(8,128)S(1)} %get-tuple-element.63, f32[128,1]{1,0:T(8,128)S(1)} %get-tuple-element.61, ...), kind=kLoop, calls=%fused_computation.120 | loop fusion | flops 4718592 | bytes 8388612 | tf_op jit(solution)/shard_map/stack | solution.py:75
  13.9 0.5 collective-permute-start.2
  14.4 1.0 collective-permute-start.3
  15.4 1.6 %collective-permute-done.2 = f32[2,3,2048]{2,1,0:T(4,128)S(1)} collective-permute-done((f32[2,3,2048]{2,1,0:T(4,128)S(1)}, f32[2,3,2048]{2,1,0:T(4,128)S(1)}, u32[]{:S(2)}, u32[]{:S(2)}) %collective-permute-start.2) | collective-permute-done | bytes 49184 | tf_op jit(solution)/shard_map/ppermute | solution.py:19
  17.1 0.7 collective-permute-done.3
  17.8 0.3 pad_maximum_fusion.1
  18.1 0.1 slice_bitcast_fusion.3
  18.2 0.4 fusion.103
  18.7 1.5 %multiply_add_fusion.3 = (f32[132,2048]{1,0:T(8,128)S(1)}, f32[132,2048]{1,0:T(8,128)S(1)}) fusion(f32[2,134,2048]{2,1,0:T(8,128)S(1)} %pad_maximum_fusion.1, f32[132,1]{1,0:T(8,128)S(1)} %get-tuple-element.58, f32[132,2047]{1,0:T(8,128)S(1)} %get-tuple-element.60, f32[132,2047]{1,0:T(8,128)S(1)} %get-tuple-element.59, f32[132,1]{1,0:T(8,128)S(1)} %get-tuple-element.57, ...), kind=kLoop, calls=%fused_computation.75 | loop fusion | flops 4866048 | bytes 8650756 | tf_op jit(solution)/shard_map/add | solution.py:92
  20.2 0.4 fusion.101
  20.6 0.1 fusion.100
  20.7 1.5 %multiply_add_fusion.2 = (f32[130,2048]{1,0:T(8,128)S(1)}, f32[130,2048]{1,0:T(8,128)S(1)}) fusion(f32[132,2048]{1,0:T(8,128)S(1)} %get-tuple-element.18, f32[130,1]{1,0:T(8,128)S(1)} %get-tuple-element.54, f32[130,2047]{1,0:T(8,128)S(1)} %get-tuple-element.56, f32[130,2047]{1,0:T(8,128)S(1)} %get-tuple-element.55, f32[130,1]{1,0:T(8,128)S(1)} %get-tuple-element.53, ...), kind=kLoop, calls=%fused_computation.74 | loop fusion | flops 4792320 | bytes 8519684 | tf_op jit(solution)/shard_map/add | solution.py:92
  22.3 0.4 fusion.99
  22.8 1.5 %add_bitcast_fusion = (f32[1,128,2048]{2,1,0:T(8,128)S(1)}, f32[128,2048]{1,0:T(8,128)S(1)}) fusion(f32[130,2048]{1,0:T(8,128)S(1)} %get-tuple-element.16, f32[128,1]{1,0:T(8,128)S(1)} %get-tuple-element.50, f32[128,2047]{1,0:T(8,128)S(1)} %get-tuple-element.52, f32[128,2047]{1,0:T(8,128)S(1)} %get-tuple-element.51, f32[128,1]{1,0:T(8,128)S(1)} %get-tuple-element.49, ...), kind=kLoop, calls=%fused_computation.119 | loop fusion | flops 4718592 | bytes 8388612 | tf_op jit(solution)/shard_map/stack | solution.py:75
  24.3 0.9 copy-done.1
  25.2 0.3 copy-done.2
  25.6 0.8 collective-permute-start.4
  26.3 0.7 collective-permute-start.5
  27.0 0.6 fusion.81
  27.7 1.3 %slice.515 = f32[128,2047]{1,0:T(8,128)} slice(f32[128,2048]{1,0:T(8,128)S(1)} %bitcast.130), slice={[0:128], [1:2048]} | slice | bytes 2096128 | tf_op jit(solution)/shard_map/jit(_roll_static)/slice | solution.py:41
  30.3 1.9 %pad_maximum_fusion.2 = f32[2,134,2048]{2,1,0:T(8,128)S(1)} fusion(f32[2,3,2048]{2,1,0:T(4,128)S(1)} %collective-permute-done.5, f32[1,128,2048]{2,1,0:T(8,128)} %bitcast.133, f32[1,128,2048]{2,1,0:T(8,128)} %copy-done.1, f32[2,3,2048]{2,1,0:T(4,128)S(1)} %collective-permute-done.4), kind=kLoop, calls=%fused_computation.3 | loop fusion | flops 1646592 | bytes 4390912 | tf_op jit(solution)/shard_map/concatenate | solution.py:17
  32.2 0.1 slice_bitcast_fusion.1
  32.3 0.4 fusion.97
  32.8 1.5 %multiply_add_fusion.1 = (f32[132,2048]{1,0:T(8,128)S(1)}, f32[132,2048]{1,0:T(8,128)S(1)}) fusion(f32[2,134,2048]{2,1,0:T(8,128)S(1)} %pad_maximum_fusion.2, f32[132,1]{1,0:T(8,128)S(1)} %get-tuple-element.46, f32[132,2047]{1,0:T(8,128)S(1)} %get-tuple-element.48, f32[132,2047]{1,0:T(8,128)S(1)} %get-tuple-element.47, f32[132,1]{1,0:T(8,128)S(1)} %get-tuple-element.45, ...), kind=kLoop, calls=%fused_computation.73 | loop fusion | flops 4866048 | bytes 8650756 | tf_op jit(solution)/shard_map/add | solution.py:92
  34.3 0.4 fusion.95
  34.7 0.1 fusion.94
  34.8 1.7 %multiply_add_fusion = (f32[130,2048]{1,0:T(8,128)S(1)}, f32[130,2048]{1,0:T(8,128)S(1)}) fusion(f32[132,2048]{1,0:T(8,128)S(1)} %get-tuple-element.12, f32[130,1]{1,0:T(8,128)S(1)} %get-tuple-element.42, f32[130,2047]{1,0:T(8,128)S(1)} %get-tuple-element.44, f32[130,2047]{1,0:T(8,128)S(1)} %get-tuple-element.43, f32[130,1]{1,0:T(8,128)S(1)} %get-tuple-element.41, ...), kind=kLoop, calls=%fused_computation.72 | loop fusion | flops 4792320 | bytes 8519684 | tf_op jit(solution)/shard_map/add | solution.py:92
  36.6 0.4 fusion.92
  37.0 0.7 copy-done.4
  37.8 0.3 copy-done.5
  38.1 4.7 %fusion.77 = (f32[16,8,2048]{2,1,0:T(8,128)}, f32[1,128,2048]{2,1,0:T(8,128)}, f32[]{:T(128)}, f32[]{:T(128)}, f32[]{:T(128)}) fusion(f32[130,2048]{1,0:T(8,128)S(1)} %get-tuple-element.10, pred[]{:T(512)} %bitcast, f32[1,128,2048]{2,1,0:T(8,128)S(1)} %copy-done, f32[1,128,2048]{2,1,0:T(8,128)S(1)} %copy-done.4, f32[128,1]{1,0:T(8,128)S(1)} %get-tuple-element.39, ...), kind=kLoop, calls=%fused_computation.123 | loop fusion | flops 12320765 | bytes 13680657 | tf_op jit(solution)/shard_map/reshape | solution.py:104
  44.0 4.9 %all-reduce.1 = (f32[1]{0:T(128)}, f32[1]{0:T(128)}) all-reduce(f32[1]{0:T(128)} %bitcast.20, f32[1]{0:T(128)} %bitcast.26), channel_id=1, replica_groups=mesh['rep'=16,'dom'=2] {'dom'}, use_global_device_ids=true, to_apply=%region_4.5 | all-reduce | flops 2 | bytes 16 | tf_op jit(solution)/shard_map/psum | solution.py:102
  48.9 0.7 select_maximum_fusion
  49.7 1.5 %pad_maximum_fusion.3 = f32[16,9,2048]{2,1,0:T(8,128)S(1)} fusion(f32[16,1,2048]{2,1,0:T(1,128)S(1)} %concatenate.111, f32[16,8,2048]{2,1,0:T(8,128)} %get-tuple-element.26), kind=kLoop, calls=%fused_computation.4 | loop fusion | flops 294912 | bytes 2359296 | tf_op jit(solution)/shard_map/concatenate | solution.py:105
  51.2 1.4 %reshape.79 = f32[1,144,2048]{2,0,1:T(1,128)S(1)} reshape(f32[16,9,2048]{2,1,0:T(8,128)S(1)} %pad_maximum_fusion.3) | data formatting | bytes 2359296 | tf_op jit(solution)/shard_map/reshape | solution.py:107
  52.6 38.6 %all_to_all.24 = f32[1,144,2048]{2,0,1:T(1,128)S(1)} all-to-all(f32[1,144,2048]{2,0,1:T(1,128)S(1)} %reshape.79), channel_id=1, replica_groups=mesh['rep'=16,'dom'=2] {'rep'}, dimensions={1} | all-to-all | bytes 2359296 | tf_op jit(solution)/shard_map/all_to_all | solution.py:106
  91.2 2.8 %reduce = f32[144,2048]{1,0:T(8,128)S(1)} reduce(f32[1,144,2048]{2,0,1:T(1,128)S(1)} %all_to_all.24, f32[]{:T(128)} %constant.76), dimensions={0}, to_apply=%all_to_all.8.reduce_sub_computation | reduce | bytes 2359300 | tf_op jit(solution)/shard_map/all_to_all | solution.py:106
  94.0 0.2 all_to_all.9
  94.2 0.4 fusion.79
  94.5 1.0 slice.518
  95.6 0.1 select_reduce_fusion.1
  95.7 1.8 %gather_fusion = f32[16,8,2048]{2,1,0:T(8,128)S(1)} fusion(f32[16,8,2048]{2,1,0:T(8,128)} %slice.518, s32[1024]{0:T(1024)S(1)} %pad_clamp_fusion), kind=kCustom, calls=%fused_computation | custom fusion | bytes 2097216 | tf_op jit(solution)/shard_map/jit(_take)/gather | solution.py:118
  97.6 1.1 broadcast_select_fusion
  98.7 4.7 %all-to-all-start.1 = ((f32[16,8,2048]{2,1,0:T(8,128)}), f32[16,8,2048]{2,1,0:T(8,128)S(1)}, u32[]{:S(2)}, u32[]{:S(2)}) async-start(f32[16,8,2048]{2,1,0:T(8,128)} %broadcast_select_fusion), calls=%async_computation.1 | async-start | bytes 2097152 | tf_op jit(solution)/shard_map/all_to_all | solution.py:119
  103.4 0.3 slice_reduce_fusion
  103.6 0.1 select_reduce_fusion
  103.8 0.6 dynamic_slice.3
  104.4 23.9 %all-to-all-done.1 = f32[16,8,2048]{2,1,0:T(8,128)S(1)} async-done(((f32[16,8,2048]{2,1,0:T(8,128)}), f32[16,8,2048]{2,1,0:T(8,128)S(1)}, u32[]{:S(2)}, u32[]{:S(2)}) %all-to-all-start.1) | async-done | bytes 1048608 | tf_op jit(solution)/shard_map/all_to_all | solution.py:119
  128.3 1.0 copy.19
  (29 shorter events, 0.8 us)
Async XLA Ops:
  0.6 1.5 %copy-start.3 = (f32[1,128,2048]{2,1,0:T(8,128)S(1)}, f32[1,128,2048]{2,1,0:T(8,128)}, u32[]{:S(2)}) copy-start(f32[1,128,2048]{2,1,0:T(8,128)} %param.7) | copy-start | bytes 3145732
  2.2 2.3 %copy-start.6 = (f32[16]{0:T(128)S(1)}, f32[16]{0:T(128)}, u32[]{:S(2)}) copy-start(f32[16]{0:T(128)} %param.9) | copy-start | bytes 196
  2.3 3.2 %collective-permute-start.1 = (f32[2,3,2048]{2,1,0:T(4,128)S(1)}, f32[2,3,2048]{2,1,0:T(4,128)S(1)}, u32[]{:S(2)}, u32[]{:S(2)}) collective-permute-start(f32[2,3,2048]{2,1,0:T(4,128)S(1)} %get-tuple-element.33), channel_id=1, source_target_pairs={{1,0},{0,1},{3,2},{2,3},{5,4},{4,5},{7,6},{6,7},{9,8},{8,9},{11,10... | collective-permute-start | bytes 147464 | tf_op jit(solution)/shard_map/ppermute | solution.py:21
  3.6 3.9 %collective-permute-start = (f32[2,3,2048]{2,1,0:T(4,128)S(1)}, f32[2,3,2048]{2,1,0:T(4,128)S(1)}, u32[]{:S(2)}, u32[]{:S(2)}) collective-permute-start(f32[2,3,2048]{2,1,0:T(4,128)S(1)} %get-tuple-element.32), channel_id=1, source_target_pairs={{0,1},{1,0},{2,3},{3,2},{4,5},{5,4},{6,7},{7,6},{8,9},{9,8},{10,11... | collective-permute-start | bytes 147464 | tf_op jit(solution)/shard_map/ppermute | solution.py:19
  13.9 3.2 %collective-permute-start.2 = (f32[2,3,2048]{2,1,0:T(4,128)S(1)}, f32[2,3,2048]{2,1,0:T(4,128)S(1)}, u32[]{:S(2)}, u32[]{:S(2)}) collective-permute-start(f32[2,3,2048]{2,1,0:T(4,128)S(1)} %get-tuple-element.30), channel_id=1, source_target_pairs={{0,1},{1,0},{2,3},{3,2},{4,5},{5,4},{6,7},{7,6},{8,9},{9,8},{10,11... | collective-permute-start | bytes 147464 | tf_op jit(solution)/shard_map/ppermute | solution.py:19
  14.4 3.3 %collective-permute-start.3 = (f32[2,3,2048]{2,1,0:T(4,128)S(1)}, f32[2,3,2048]{2,1,0:T(4,128)S(1)}, u32[]{:S(2)}, u32[]{:S(2)}) collective-permute-start(f32[2,3,2048]{2,1,0:T(4,128)S(1)} %get-tuple-element.31), channel_id=1, source_target_pairs={{1,0},{0,1},{3,2},{2,3},{5,4},{4,5},{7,6},{6,7},{9,8},{8,9},{11,10... | collective-permute-start | bytes 147464 | tf_op jit(solution)/shard_map/ppermute | solution.py:21
  24.2 1.0 copy-start.1
  24.2 1.3 %copy-start.2 = (f32[128,2048]{1,0:T(8,128)}, f32[128,2048]{1,0:T(8,128)S(1)}, u32[]{:S(2)}) copy-start(f32[128,2048]{1,0:T(8,128)S(1)} %get-tuple-element.15) | copy-start | bytes 3145732
  24.3 2.8 %copy-start.7 = (s32[16]{0:T(128)S(1)}, s32[16]{0:T(128)}, u32[]{:S(2)}) copy-start(s32[16]{0:T(128)} %param.11) | copy-start | bytes 196
  24.3 3.4 %copy-start = (f32[1,128,2048]{2,1,0:T(8,128)S(1)}, f32[1,128,2048]{2,1,0:T(8,128)}, u32[]{:S(2)}) copy-start(f32[1,128,2048]{2,1,0:T(8,128)} %param.6) | copy-start | bytes 3145732
  25.6 4.7 %collective-permute-start.4 = (f32[2,3,2048]{2,1,0:T(4,128)S(1)}, f32[2,3,2048]{2,1,0:T(4,128)S(1)}, u32[]{:S(2)}, u32[]{:S(2)}) collective-permute-start(f32[2,3,2048]{2,1,0:T(4,128)S(1)} %get-tuple-element.28), channel_id=1, source_target_pairs={{0,1},{1,0},{2,3},{3,2},{4,5},{5,4},{6,7},{7,6},{8,9},{9,8},{10,11... | collective-permute-start | bytes 147464 | tf_op jit(solution)/shard_map/ppermute | solution.py:19
  26.3 4.0 %collective-permute-start.5 = (f32[2,3,2048]{2,1,0:T(4,128)S(1)}, f32[2,3,2048]{2,1,0:T(4,128)S(1)}, u32[]{:S(2)}, u32[]{:S(2)}) collective-permute-start(f32[2,3,2048]{2,1,0:T(4,128)S(1)} %get-tuple-element.29), channel_id=1, source_target_pairs={{1,0},{0,1},{3,2},{2,3},{5,4},{4,5},{7,6},{6,7},{9,8},{8,9},{11,10... | collective-permute-start | bytes 147464 | tf_op jit(solution)/shard_map/ppermute | solution.py:21
  36.5 1.2 copy-start.4
  36.5 1.5 %copy-start.5 = (f32[128,2047]{1,0:T(8,128)S(1)}, f32[128,2047]{1,0:T(8,128)}, u32[]{:S(2)}) copy-start(f32[128,2047]{1,0:T(8,128)} %slice.515) | copy-start | bytes 3144196
  98.7 29.6 %all-to-all-start.1 = ((f32[16,8,2048]{2,1,0:T(8,128)}), f32[16,8,2048]{2,1,0:T(8,128)S(1)}, u32[]{:S(2)}, u32[]{:S(2)}) async-start(f32[16,8,2048]{2,1,0:T(8,128)} %broadcast_select_fusion), calls=%async_computation.1 | async-start | bytes 2097152 | tf_op jit(solution)/shard_map/all_to_all | solution.py:119
where the time goes:
time: 130 us; the launch traced here: 129 us
  blocking collectives  43.5 us (33%)
  waiting for transfers between devices  28.7 us (22%)
  other arithmetic  27.5 us (21%)
  local copies, waits for them, and re-layouts  16.2 us (12%)
  starting transfers between devices  9.18 us (7%)
  between operations  4.24 us (3%)
    all_to_all x1, blocking collectives, body(): lax.all_to_all(outgoing.reshape(1, -1, width), 'rep', split_axis=1, conca...  38.6 us
    all_to_all x1, waiting for transfers between devices, body(): lax.all_to_all(ordered, 'rep', split_axis=0, concat_axis=1, tiled=True)  23.9 us
    add x6, other arithmetic, body(): current = current + step_size * moment  9.39 us
    psum x1, blocking collectives, body(): change, action = lax.psum((change_part[None], action_part[None]), 'dom')  4.91 us
    unnamed x18, local copies, waits for them, and re-layouts  4.81 us
    reshape x1, other arithmetic, body(): blocks = field_out.reshape(members, -1, width)  4.67 us
    all_to_all x1, starting transfers between devices, body(): lax.all_to_all(ordered, 'rep', split_axis=0, concat_axis=1, tiled=True)  4.66 us
    slice x16, local copies, waits for them, and re-layouts, force_rows(): jnp.roll(centre, 1, 1) + jnp.roll(centre, -1, 1)  3.78 us
  transfers between devices with their start and end apart: 7, of which 5 were waited for; matrix products, arithmetic and copies ran while one was open for 3% of the time, Pallas kernels for 0%

commit v1 on v0

--- a/solution.py
+++ b/solution.py
@@ -116,7 +116,10 @@
     ladder_all = jnp.sum(jnp.where(onehot, actions[None, :], 0.0), 1) / sites_total
     ladder = lax.dynamic_slice_in_dim(ladder_all, lax.axis_index("rep"), 1)
     ordered = jnp.take(received, holder, axis=0)
-    returned = lax.all_to_all(ordered, "rep", split_axis=0, concat_axis=1, tiled=True)
+    size = lax.axis_size("rep")
+    shards = jnp.stack(jnp.split(ordered, size, axis=0), axis=0)
+    shards = lax.all_to_all(shards, "rep", split_axis=0, concat_axis=0)
+    returned = jnp.concatenate(shards, axis=1)
     return (field_out[None], returned, new_label[None], change, ladder)
 
 

time: 130 us -> 139 us (1.069)
  local copies, waits for them, and re-layouts: 16.2 us -> 26.4 us
    unnamed x18 -> x33, local copies, waits for them, and re-layouts: 4.81 us -> 14.3 us
where the time goes in v1:
time: 139 us
  blocking collectives  43.5 us (31%)
  waiting for transfers between devices  28.7 us (21%)
  other arithmetic  26.6 us (19%)
  local copies, waits for them, and re-layouts  26.4 us (19%)
  starting transfers between devices  9.18 us (7%)
  between operations  4.26 us (3%)
    all_to_all x1, blocking collectives, body(): lax.all_to_all(outgoing.reshape(1, -1, width), 'rep', split_axis=1, conca...  38.6 us
    all_to_all x1, waiting for transfers between devices, body(): shards = lax.all_to_all(shards, 'rep', split_axis=0, concat_axis=0)  23.9 us
    unnamed x33, local copies, waits for them, and re-layouts  14.3 us
    add x6, other arithmetic, body(): current = current + step_size * moment  9.39 us
    psum x1, blocking collectives, body(): change, action = lax.psum((change_part[None], action_part[None]), 'dom')  4.91 us
    reshape x1, other arithmetic, body(): blocks = field_out.reshape(members, -1, width)  4.67 us
    all_to_all x1, starting transfers between devices, body(): shards = lax.all_to_all(shards, 'rep', split_axis=0, concat_axis=0)  4.66 us
    slice x16, local copies, waits for them, and re-layouts, force_rows(): jnp.roll(centre, 1, 1) + jnp.roll(centre, -1, 1)  3.78 us
  transfers between devices with their start and end apart: 7, of which 5 were waited for; matrix products, arithmetic and copies ran while one was open for 3% of the time, Pallas kernels for 0%

profile of v1, /device:TPU:9, one launch (start us, length us, event | category | flops | bytes accessed | tf_op | source)
XLA Modules:
  0.0 138.6 jit_solution(5427600131527151947)
XLA Ops:
  0.6 1.4 %constant_dynamic-update-slice_fusion.1 = f32[2,128,2048]{2,1,0:T(8,128)S(1)} fusion(f32[1,128,2048]{2,1,0:T(8,128)} %param.6), kind=kLoop, calls=%fused_computation.162 | loop fusion | bytes 2097152
  2.3 1.3 collective-permute-start.1
  4.5 0.6 fusion.96
  5.1 0.4 collective-permute-done.1
  5.5 2.0 %collective-permute-done = f32[2,3,2048]{2,1,0:T(4,128)S(1)} collective-permute-done((f32[2,3,2048]{2,1,0:T(4,128)S(1)}, f32[2,3,2048]{2,1,0:T(4,128)S(1)}, u32[]{:S(2)}, u32[]{:S(2)}) %collective-permute-start) | collective-permute-done | bytes 49184 | tf_op jit(solution)/shard_map/ppermute | solution.py:19
  8.0 0.4 fusion.125
  8.4 1.5 %multiply_add_fusion.5 = (f32[132,2048]{1,0:T(8,128)S(1)}, f32[132,2048]{1,0:T(8,128)S(1)}) fusion(f32[2,134,2048]{2,1,0:T(8,128)S(1)} %pad_maximum_fusion, f32[132,1]{1,0:T(8,128)S(1)} %get-tuple-element.70, f32[132,2047]{1,0:T(8,128)S(1)} %get-tuple-element.72, f32[132,2047]{1,0:T(8,128)S(1)} %get-tuple-element.71, f32[132,1]{1,0:T(8,128)S(1)} %get-tuple-element.69, ...), kind=kLoop, calls=%fused_computation.77 | loop fusion | flops 4866048 | bytes 8650756 | tf_op jit(solution)/shard_map/add | solution.py:92
  10.0 0.4 fusion.123
  10.5 1.5 %multiply_add_fusion.4 = (f32[130,2048]{1,0:T(8,128)S(1)}, f32[130,2048]{1,0:T(8,128)S(1)}) fusion(f32[132,2048]{1,0:T(8,128)S(1)} %get-tuple-element.24, f32[130,1]{1,0:T(8,128)S(1)} %get-tuple-element.66, f32[130,2047]{1,0:T(8,128)S(1)} %get-tuple-element.68, f32[130,2047]{1,0:T(8,128)S(1)} %get-tuple-element.67, f32[130,1]{1,0:T(8,128)S(1)} %get-tuple-element.65, ...), kind=kLoop, calls=%fused_computation.76 | loop fusion | flops 4792320 | bytes 8519684 | tf_op jit(solution)/shard_map/add | solution.py:92
  12.0 0.4 fusion.121
  12.5 1.5 %add_bitcast_fusion.1 = (f32[1,128,2048]{2,1,0:T(8,128)S(1)}, f32[128,2048]{1,0:T(8,128)S(1)}) fusion(f32[130,2048]{1,0:T(8,128)S(1)} %get-tuple-element.22, f32[128,1]{1,0:T(8,128)S(1)} %get-tuple-element.62, f32[128,2047]{1,0:T(8,128)S(1)} %get-tuple-element.64, f32[128,2047]{1,0:T(8,128)S(1)} %get-tuple-element.63, f32[128,1]{1,0:T(8,128)S(1)} %get-tuple-element.61, ...), kind=kLoop, calls=%fused_computation.120 | loop fusion | flops 4718592 | bytes 8388612 | tf_op jit(solution)/shard_map/stack | solution.py:75
  14.0 0.5 collective-permute-start.2
  14.6 1.0 collective-permute-start.3
  15.5 1.6 %collective-permute-done.2 = f32[2,3,2048]{2,1,0:T(4,128)S(1)} collective-permute-done((f32[2,3,2048]{2,1,0:T(4,128)S(1)}, f32[2,3,2048]{2,1,0:T(4,128)S(1)}, u32[]{:S(2)}, u32[]{:S(2)}) %collective-permute-start.2) | collective-permute-done | bytes 49184 | tf_op jit(solution)/shard_map/ppermute | solution.py:19
  17.2 0.7 collective-permute-done.3
  18.3 0.4 fusion.119
  18.8 1.5 %multiply_add_fusion.3 = (f32[132,2048]{1,0:T(8,128)S(1)}, f32[132,2048]{1,0:T(8,128)S(1)}) fusion(f32[2,134,2048]{2,1,0:T(8,128)S(1)} %pad_maximum_fusion.1, f32[132,1]{1,0:T(8,128)S(1)} %get-tuple-element.58, f32[132,2047]{1,0:T(8,128)S(1)} %get-tuple-element.60, f32[132,2047]{1,0:T(8,128)S(1)} %get-tuple-element.59, f32[132,1]{1,0:T(8,128)S(1)} %get-tuple-element.57, ...), kind=kLoop, calls=%fused_computation.75 | loop fusion | flops 4866048 | bytes 8650756 | tf_op jit(solution)/shard_map/add | solution.py:92
  20.3 0.4 fusion.117
  20.9 1.5 %multiply_add_fusion.2 = (f32[130,2048]{1,0:T(8,128)S(1)}, f32[130,2048]{1,0:T(8,128)S(1)}) fusion(f32[132,2048]{1,0:T(8,128)S(1)} %get-tuple-element.18, f32[130,1]{1,0:T(8,128)S(1)} %get-tuple-element.54, f32[130,2047]{1,0:T(8,128)S(1)} %get-tuple-element.56, f32[130,2047]{1,0:T(8,128)S(1)} %get-tuple-element.55, f32[130,1]{1,0:T(8,128)S(1)} %get-tuple-element.53, ...), kind=kLoop, calls=%fused_computation.74 | loop fusion | flops 4792320 | bytes 8519684 | tf_op jit(solution)/shard_map/add | solution.py:92
  22.4 0.4 fusion.115
  22.9 1.5 %add_bitcast_fusion = (f32[1,128,2048]{2,1,0:T(8,128)S(1)}, f32[128,2048]{1,0:T(8,128)S(1)}) fusion(f32[130,2048]{1,0:T(8,128)S(1)} %get-tuple-element.16, f32[128,1]{1,0:T(8,128)S(1)} %get-tuple-element.50, f32[128,2047]{1,0:T(8,128)S(1)} %get-tuple-element.52, f32[128,2047]{1,0:T(8,128)S(1)} %get-tuple-element.51, f32[128,1]{1,0:T(8,128)S(1)} %get-tuple-element.49, ...), kind=kLoop, calls=%fused_computation.119 | loop fusion | flops 4718592 | bytes 8388612 | tf_op jit(solution)/shard_map/stack | solution.py:75
  24.4 0.9 copy-done.1
  25.3 0.3 copy-done.2
  25.7 0.8 collective-permute-start.4
  26.4 0.7 collective-permute-start.5
  27.1 0.6 fusion.97
  27.8 1.3 slice.515
  30.4 1.9 %pad_maximum_fusion.2 = f32[2,134,2048]{2,1,0:T(8,128)S(1)} fusion(f32[2,3,2048]{2,1,0:T(4,128)S(1)} %collective-permute-done.5, f32[1,128,2048]{2,1,0:T(8,128)} %bitcast.197, f32[1,128,2048]{2,1,0:T(8,128)} %copy-done.1, f32[2,3,2048]{2,1,0:T(4,128)S(1)} %collective-permute-done.4), kind=kLoop, calls=%fused_computation.3 | loop fusion | flops 1646592 | bytes 4390912 | tf_op jit(solution)/shard_map/concatenate | solution.py:17
  32.4 0.4 fusion.113
  32.9 1.5 %multiply_add_fusion.1 = (f32[132,2048]{1,0:T(8,128)S(1)}, f32[132,2048]{1,0:T(8,128)S(1)}) fusion(f32[2,134,2048]{2,1,0:T(8,128)S(1)} %pad_maximum_fusion.2, f32[132,1]{1,0:T(8,128)S(1)} %get-tuple-element.46, f32[132,2047]{1,0:T(8,128)S(1)} %get-tuple-element.48, f32[132,2047]{1,0:T(8,128)S(1)} %get-tuple-element.47, f32[132,1]{1,0:T(8,128)S(1)} %get-tuple-element.45, ...), kind=kLoop, calls=%fused_computation.73 | loop fusion | flops 4866048 | bytes 8650756 | tf_op jit(solution)/shard_map/add | solution.py:92
  34.4 0.4 fusion.111
  34.9 1.7 %multiply_add_fusion = (f32[130,2048]{1,0:T(8,128)S(1)}, f32[130,2048]{1,0:T(8,128)S(1)}) fusion(f32[132,2048]{1,0:T(8,128)S(1)} %get-tuple-element.12, f32[130,1]{1,0:T(8,128)S(1)} %get-tuple-element.42, f32[130,2047]{1,0:T(8,128)S(1)} %get-tuple-element.44, f32[130,2047]{1,0:T(8,128)S(1)} %get-tuple-element.43, f32[130,1]{1,0:T(8,128)S(1)} %get-tuple-element.41, ...), kind=kLoop, calls=%fused_computation.72 | loop fusion | flops 4792320 | bytes 8519684 | tf_op jit(solution)/shard_map/add | solution.py:92
  36.7 0.4 fusion.108
  37.2 0.7 copy-done.4
  38.2 4.7 %fusion.77 = (f32[16,8,2048]{2,1,0:T(8,128)}, f32[1,128,2048]{2,1,0:T(8,128)}, f32[]{:T(128)}, f32[]{:T(128)}, f32[]{:T(128)}) fusion(f32[130,2048]{1,0:T(8,128)S(1)} %get-tuple-element.10, pred[]{:T(512)} %bitcast, f32[1,128,2048]{2,1,0:T(8,128)S(1)} %copy-done, f32[1,128,2048]{2,1,0:T(8,128)S(1)} %copy-done.4, f32[128,1]{1,0:T(8,128)S(1)} %get-tuple-element.39, ...), kind=kLoop, calls=%fused_computation.123 | loop fusion | flops 12320765 | bytes 13680657 | tf_op jit(solution)/shard_map/reshape | solution.py:104
  44.1 4.9 %all-reduce.1 = (f32[1]{0:T(128)}, f32[1]{0:T(128)}) all-reduce(f32[1]{0:T(128)} %bitcast.20, f32[1]{0:T(128)} %bitcast.42), channel_id=1, replica_groups=mesh['rep'=16,'dom'=2] {'dom'}, use_global_device_ids=true, to_apply=%region_4.5 | all-reduce | flops 2 | bytes 16 | tf_op jit(solution)/shard_map/psum | solution.py:102
  49.0 0.7 select_maximum_fusion
  49.8 1.5 %pad_maximum_fusion.3 = f32[16,9,2048]{2,1,0:T(8,128)S(1)} fusion(f32[16,1,2048]{2,1,0:T(1,128)S(1)} %concatenate.111, f32[16,8,2048]{2,1,0:T(8,128)} %get-tuple-element.26), kind=kLoop, calls=%fused_computation.4 | loop fusion | flops 294912 | bytes 2359296 | tf_op jit(solution)/shard_map/concatenate | solution.py:105
  51.3 1.4 %reshape.80 = f32[1,144,2048]{2,0,1:T(1,128)S(1)} reshape(f32[16,9,2048]{2,1,0:T(8,128)S(1)} %pad_maximum_fusion.3) | data formatting | bytes 2359296 | tf_op jit(solution)/shard_map/reshape | solution.py:107
  52.8 38.6 %all_to_all.17 = f32[1,144,2048]{2,0,1:T(1,128)S(1)} all-to-all(f32[1,144,2048]{2,0,1:T(1,128)S(1)} %reshape.80), channel_id=1, replica_groups=mesh['rep'=16,'dom'=2] {'rep'}, dimensions={1} | all-to-all | bytes 2359296 | tf_op jit(solution)/shard_map/all_to_all | solution.py:106
  91.3 2.8 %reduce = f32[144,2048]{1,0:T(8,128)S(1)} reduce(f32[1,144,2048]{2,0,1:T(1,128)S(1)} %all_to_all.17, f32[]{:T(128)} %constant.76), dimensions={0}, to_apply=%all_to_all.12.reduce_sub_computation | reduce | bytes 2359300 | tf_op jit(solution)/shard_map/all_to_all | solution.py:106
  94.3 0.4 fusion.95
  94.7 1.1 slice.518
  95.9 1.8 %gather_fusion = f32[16,8,2048]{2,1,0:T(8,128)S(1)} fusion(f32[16,8,2048]{2,1,0:T(8,128)} %slice.518, s32[1024]{0:T(1024)S(1)} %pad_clamp_fusion), kind=kCustom, calls=%fused_computation | custom fusion | bytes 2097216 | tf_op jit(solution)/shard_map/jit(_take)/gather | solution.py:118
  97.9 0.6 fusion.94
  98.6 0.6 fusion.93
  99.2 0.6 fusion.92
  99.8 0.6 fusion.91
  100.5 0.6 fusion.90
  101.1 0.6 fusion.89
  101.7 0.6 fusion.88
  102.4 0.6 fusion.87
  103.0 0.6 fusion.86
  103.6 0.6 fusion.85
  104.3 0.6 fusion.84
  104.9 0.6 fusion.83
  105.5 0.6 fusion.82
  106.2 0.6 fusion.81
  106.8 0.6 fusion.80
  107.4 0.6 fusion.79
  108.1 4.7 %all-to-all-start.1 = ((f32[16,1,8,2048]{3,2,1,0:T(8,128)}), f32[16,1,8,2048]{3,2,1,0:T(8,128)S(1)}, u32[]{:S(2)}, u32[]{:S(2)}) async-start(f32[16,1,8,2048]{3,2,1,0:T(8,128)} %fusion.79), calls=%async_computation.1 | async-start | bytes 2097152 | tf_op jit(solution)/shard_map/all_to_all | solution.py:121
  113.1 0.6 dynamic_slice.3
  113.7 23.9 %all-to-all-done.1 = f32[16,1,8,2048]{3,2,1,0:T(8,128)S(1)} async-done(((f32[16,1,8,2048]{3,2,1,0:T(8,128)}), f32[16,1,8,2048]{3,2,1,0:T(8,128)S(1)}, u32[]{:S(2)}, u32[]{:S(2)}) %all-to-all-start.1) | async-done | bytes 1048608 | tf_op jit(solution)/shard_map/all_to_all | solution.py:121
  137.7 1.0 copy.48
  (45 shorter events, 3.6 us)
Async XLA Ops:
  0.6 1.5 %copy-start.3 = (f32[1,128,2048]{2,1,0:T(8,128)S(1)}, f32[1,128,2048]{2,1,0:T(8,128)}, u32[]{:S(2)}) copy-start(f32[1,128,2048]{2,1,0:T(8,128)} %param.7) | copy-start | bytes 3145732
  2.2 2.3 %copy-start.6 = (f32[16]{0:T(128)S(1)}, f32[16]{0:T(128)}, u32[]{:S(2)}) copy-start(f32[16]{0:T(128)} %param.9) | copy-start | bytes 196
  2.3 3.2 %collective-permute-start.1 = (f32[2,3,2048]{2,1,0:T(4,128)S(1)}, f32[2,3,2048]{2,1,0:T(4,128)S(1)}, u32[]{:S(2)}, u32[]{:S(2)}) collective-permute-start(f32[2,3,2048]{2,1,0:T(4,128)S(1)} %get-tuple-element.33), channel_id=1, source_target_pairs={{1,0},{0,1},{3,2},{2,3},{5,4},{4,5},{7,6},{6,7},{9,8},{8,9},{11,10... | collective-permute-start | bytes 147464 | tf_op jit(solution)/shard_map/ppermute | solution.py:21
  3.6 3.9 %collective-permute-start = (f32[2,3,2048]{2,1,0:T(4,128)S(1)}, f32[2,3,2048]{2,1,0:T(4,128)S(1)}, u32[]{:S(2)}, u32[]{:S(2)}) collective-permute-start(f32[2,3,2048]{2,1,0:T(4,128)S(1)} %get-tuple-element.32), channel_id=1, source_target_pairs={{0,1},{1,0},{2,3},{3,2},{4,5},{5,4},{6,7},{7,6},{8,9},{9,8},{10,11... | collective-permute-start | bytes 147464 | tf_op jit(solution)/shard_map/ppermute | solution.py:19
  14.0 3.2 %collective-permute-start.2 = (f32[2,3,2048]{2,1,0:T(4,128)S(1)}, f32[2,3,2048]{2,1,0:T(4,128)S(1)}, u32[]{:S(2)}, u32[]{:S(2)}) collective-permute-start(f32[2,3,2048]{2,1,0:T(4,128)S(1)} %get-tuple-element.30), channel_id=1, source_target_pairs={{0,1},{1,0},{2,3},{3,2},{4,5},{5,4},{6,7},{7,6},{8,9},{9,8},{10,11... | collective-permute-start | bytes 147464 | tf_op jit(solution)/shard_map/ppermute | solution.py:19
  14.6 3.3 %collective-permute-start.3 = (f32[2,3,2048]{2,1,0:T(4,128)S(1)}, f32[2,3,2048]{2,1,0:T(4,128)S(1)}, u32[]{:S(2)}, u32[]{:S(2)}) collective-permute-start(f32[2,3,2048]{2,1,0:T(4,128)S(1)} %get-tuple-element.31), channel_id=1, source_target_pairs={{1,0},{0,1},{3,2},{2,3},{5,4},{4,5},{7,6},{6,7},{9,8},{8,9},{11,10... | collective-permute-start | bytes 147464 | tf_op jit(solution)/shard_map/ppermute | solution.py:21
  24.3 1.0 copy-start.1
  24.4 1.3 copy-start.2
  24.4 2.8 %copy-start.7 = (s32[16]{0:T(128)S(1)}, s32[16]{0:T(128)}, u32[]{:S(2)}) copy-start(s32[16]{0:T(128)} %param.11) | copy-start | bytes 196
  24.4 3.4 %copy-start = (f32[1,128,2048]{2,1,0:T(8,128)S(1)}, f32[1,128,2048]{2,1,0:T(8,128)}, u32[]{:S(2)}) copy-start(f32[1,128,2048]{2,1,0:T(8,128)} %param.6) | copy-start | bytes 3145732
  25.7 4.7 %collective-permute-start.4 = (f32[2,3,2048]{2,1,0:T(4,128)S(1)}, f32[2,3,2048]{2,1,0:T(4,128)S(1)}, u32[]{:S(2)}, u32[]{:S(2)}) collective-permute-start(f32[2,3,2048]{2,1,0:T(4,128)S(1)} %get-tuple-element.28), channel_id=1, source_target_pairs={{0,1},{1,0},{2,3},{3,2},{4,5},{5,4},{6,7},{7,6},{8,9},{9,8},{10,11... | collective-permute-start | bytes 147464 | tf_op jit(solution)/shard_map/ppermute | solution.py:19
  26.4 4.0 %collective-permute-start.5 = (f32[2,3,2048]{2,1,0:T(4,128)S(1)}, f32[2,3,2048]{2,1,0:T(4,128)S(1)}, u32[]{:S(2)}, u32[]{:S(2)}) collective-permute-start(f32[2,3,2048]{2,1,0:T(4,128)S(1)} %get-tuple-element.29), channel_id=1, source_target_pairs={{1,0},{0,1},{3,2},{2,3},{5,4},{4,5},{7,6},{6,7},{9,8},{8,9},{11,10... | collective-permute-start | bytes 147464 | tf_op jit(solution)/shard_map/ppermute | solution.py:21
  36.6 1.2 copy-start.4
  36.7 1.5 %copy-start.5 = (f32[128,2047]{1,0:T(8,128)S(1)}, f32[128,2047]{1,0:T(8,128)}, u32[]{:S(2)}) copy-start(f32[128,2047]{1,0:T(8,128)} %slice.515) | copy-start | bytes 3144196
  108.1 29.6 %all-to-all-start.1 = ((f32[16,1,8,2048]{3,2,1,0:T(8,128)}), f32[16,1,8,2048]{3,2,1,0:T(8,128)S(1)}, u32[]{:S(2)}, u32[]{:S(2)}) async-start(f32[16,1,8,2048]{3,2,1,0:T(8,128)} %fusion.79), calls=%async_computation.1 | async-start | bytes 2097152 | tf_op jit(solution)/shard_map/all_to_all | solution.py:121
